TPU v7x, 128 devices: a whole 4x4x4 slice. The times are simulated.
128 devices in a mesh: row: 8 (over z, core), col: 16 (over x, y).
Axes of the slice: x: 4, y: 4, z: 4, core: 2. Of those that a mesh axis runs over, the one named last changes fastest.
Arguments:
- hessian_inverse: float32 [12288, 12288], P('row', 'col'), as said below
- weight: bfloat16 [12288, 4096], P('row', 'col'), may hold values from -6 to 6
- pruned: int32 [2, 512], replicated, may hold values from 0 to 12287, as said below
Outputs:
- hessian_after: float32 [12288, 12288], P('row', 'col')
- weight_after: bfloat16 [12288, 4096], P('row', 'col')
Inputs may be any that keep to these rules, and one draw needn't show every extreme that they name: `hessian_inverse`: symmetric and positive definite. `pruned`: all 1024 channel numbers are distinct.
All inputs are finite; a program needn't handle non-finite values.
Results may differ from a plain program's by a relative error of at most 0.001.
Values sent between devices are 32-bit elements; how exact they have to be, the bound alone decides.
No kernel may reach another device: no remote copies, remote signals or barrier semaphores. Data moves between devices by JAX's collectives and lax.ppermute only.
A program may use at most 128 MiB of HBM per device.

v0:
```python
import jax
import jax.numpy as jnp
from jax import lax
from jax.sharding import PartitionSpec as P

PANELS = 2


def contract_rows(gains, rows):
    return lax.dot_general(
        gains,
        rows,
        (((0,), (0,)), ((), ())),
        precision=lax.Precision.HIGHEST,
        preferred_element_type=jnp.float32,
    )


def solve_pivot(factor, rhs):
    half = lax.linalg.triangular_solve(factor, rhs, left_side=True, lower=True)
    return lax.linalg.triangular_solve(factor, half, left_side=True, lower=True, transpose_a=True)


def locate(listed, start, count):
    local_ids = listed - start
    valid = (local_ids >= 0) & (local_ids < count)
    clipped = jnp.clip(local_ids, 0, count - 1)
    marked = jnp.zeros((count,), jnp.float32).at[clipped].max(valid.astype(jnp.float32)) > 0.5
    return (clipped, valid, marked)


def per_device(hessian_inverse, weight, pruned):
    row_count = hessian_inverse.shape[0]
    col_count = hessian_inverse.shape[1]
    row_start = lax.axis_index("row") * row_count
    col_start = lax.axis_index("col") * col_count
    inverse = hessian_inverse
    slab = weight.astype(jnp.float32)
    for panel in range(PANELS):
        listed = pruned[panel]
        row_pick, row_valid, row_marked = locate(listed, row_start, row_count)
        col_pick, col_valid, col_marked = locate(listed, col_start, col_count)
        mine_rows = jnp.where(row_valid[:, None], jnp.take(inverse, row_pick, axis=0), 0.0)
        mine_slab = jnp.where(row_valid[:, None], jnp.take(slab, row_pick, axis=0), 0.0)
        panel_rows, slab_rows = lax.psum((mine_rows, mine_slab), "row")
        panel_pivot = jnp.where(col_valid[None, :], jnp.take(panel_rows, col_pick, axis=1), 0.0)
        pivot = lax.psum(panel_pivot, "col")
        factor = jnp.linalg.cholesky(pivot)
        mine_cols = jnp.where(col_valid[None, :], jnp.take(inverse, col_pick, axis=1), 0.0)
        columns = lax.psum(mine_cols, "col")
        gains = solve_pivot(factor, columns.T)
        slab = slab - contract_rows(gains, slab_rows)
        slab = jnp.where(row_marked[:, None], 0.0, slab)
        inverse = inverse - contract_rows(gains, panel_rows)
        inverse = jnp.where(row_marked[:, None] | col_marked[None, :], 0.0, inverse)
    return (inverse, slab.astype(jnp.bfloat16))


def solution(mesh):
    in_specs = (P("row", "col"), P("row", "col"), P())
    out_specs = (P("row", "col"), P("row", "col"))
    return jax.shard_map(
        per_device, mesh=mesh, in_specs=in_specs, out_specs=out_specs, check_vma=False
    )
```

profile of v0, /device:TPU:1, one launch (start us, length us, event | category | flops | bytes accessed | tf_op | source)
XLA Modules:
  0.0 719.2 jit_solution(886581179572580454)
XLA Ops:
  10.1 4.8 gather_fusion
  19.7 6.0 copy.13
  25.7 6.0 gather_fusion.2
  33.8 53.3 %all-reduce.16.cloned.1.call-done = (f32[512,768]{1,0:T(8,128)}, f32[512,256]{1,0:T(8,128)}) async-done(((f32[512,768]{1,0:T(8,128)}, f32[512,256]{1,0:T(8,128)}), (f32[512,768]{1,0:T(8,128)}, f32[512,256]{1,0:T(8,128)})) %all-reduce.16.cloned.1.call-update) | async-done | bytes 2097168 | tf_op jit(solution)/shard_map/psum | solution.py:45
  99.8 96.6 %all-reduce.12.cloned.1.call-done = (f32[512,1536]{1,0:T(8,128)}, f32[512,512]{0,1:T(8,128)}) async-done(((f32[512,1536]{1,0:T(8,128)}, f32[512,512]{0,1:T(8,128)}), (f32[512,1536]{1,0:T(8,128)}, f32[512,512]{0,1:T(8,128)})) %all-reduce.12.cloned.1.call-update) | async-done | bytes 4194320 | tf_op jit(solution)/shard_map/psum | solution.py:50
  198.3 11.7 %cholesky.286 = f32[128,128]{1,0:T(8,128)S(1)} custom-call(f32[128,128]{1,0:T(8,128)S(1)} %cholesky.426), custom_call_target="Cholesky" | custom-call | tf_op jit(solution)/shard_map/jit(cholesky)/cholesky | solution.py:48
  210.2 9.8 %custom-call.31 = f32[1,128,128]{1,2,0:T(8,128)S(1)} custom-call(f32[1,128,128]{2,1,0:T(8,128)S(1)} %get-tuple-element.100), custom_call_target="InvertDiagBlocksLowerTriangular" | custom-call | tf_op jit(solution)/shard_map/jit(cholesky)/cholesky | solution.py:48
  220.6 11.7 %cholesky.305 = f32[128,128]{1,0:T(8,128)S(1)} custom-call(f32[128,128]{1,0:T(8,128)S(1)} %cholesky.430), custom_call_target="Cholesky" | custom-call | tf_op jit(solution)/shard_map/jit(cholesky)/cholesky | solution.py:48
  232.4 10.2 %custom-call.32 = f32[1,128,128]{1,2,0:T(8,128)S(1)} custom-call(f32[1,128,128]{2,1,0:T(8,128)S(1)} %get-tuple-element.97), custom_call_target="InvertDiagBlocksLowerTriangular" | custom-call | tf_op jit(solution)/shard_map/jit(cholesky)/cholesky | solution.py:48
  243.2 11.7 %cholesky.326 = f32[128,128]{1,0:T(8,128)S(1)} custom-call(f32[128,128]{1,0:T(8,128)S(1)} %cholesky.435), custom_call_target="Cholesky" | custom-call | tf_op jit(solution)/shard_map/jit(cholesky)/cholesky | solution.py:48
  255.0 9.8 %custom-call.33 = f32[1,128,128]{1,2,0:T(8,128)S(1)} custom-call(f32[1,128,128]{2,1,0:T(8,128)S(1)} %get-tuple-element.94), custom_call_target="InvertDiagBlocksLowerTriangular" | custom-call | tf_op jit(solution)/shard_map/jit(cholesky)/cholesky | solution.py:48
  265.4 11.7 %cholesky.343 = f32[128,128]{1,0:T(8,128)S(1)} custom-call(f32[128,128]{1,0:T(8,128)S(1)} %convolution_subtract_fusion.19), custom_call_target="Cholesky" | custom-call | tf_op jit(solution)/shard_map/jit(cholesky)/cholesky | solution.py:48
  282.0 7.6 %while.8 = (s32[]{:T(128)}, f32[512,512]{1,0:T(8,128)S(1)}, s32[4,2]{0,1:T(2,128)S(1)}, f32[4,128,128]{2,1,0:T(8,128)S(1)}, s32[]{:T(128)}) while((s32[]{:T(128)}, f32[512,512]{1,0:T(8,128)S(1)}, s32[4,2]{0,1:T(2,128)S(1)}, f32[4,128,128]{2,1,0:T(8,128)S(1)}, s32[]{:T(128)}) %tuple.80), condition=%wide.while_cond.1, body=%wide.while_body.1.sunk | while | flops 2 | bytes 131189 | solution.py:21
  289.6 39.3 %custom-call.35 = f32[4,128,128]{1,2,0:T(8,128)S(1)} custom-call(f32[4,128,128]{2,1,0:T(8,128)S(1)} %get-tuple-element.38), custom_call_target="InvertDiagBlocksLowerTriangular" | custom-call | tf_op jit(solution)/shard_map/triangular_solve/custom-call.8 | solution.py:21
  345.3 10.7 %subtract_select_fusion.1 = f32[1536,768]{1,0:T(8,128)} fusion(f32[1536,768]{1,0:T(8,128)S(1)} %bitcast.167, f32[512,768]{1,0:T(8,128)S(1)} %copy-done.2, pred[768]{0:T(1024)(128)(4,1)S(1)} %broadcast_compare_fusion.2, pred[1536]{0:T(1024)(128)(4,1)S(1)} %broadcast_compare_fusion, f32[128,1536]{1,0:T(8,128)S(1)} %fusion.83, f32[128,1536]{1,0:T(8,128)S(1)} %fusion.81, ...), kind=kOutput, calls=%fused_computation.17 | convolution fusion | flops 7253655552 | bytes 14158080 | tf_op jit(solution)/shard_map/dot_general | solution.py:10
  356.0 5.5 fusion.3
  361.5 5.4 gather_fusion.3
  371.6 6.0 copy.16
  377.7 6.0 gather_fusion.5
  385.8 50.2 %all-reduce.14.cloned.1.call-done = (f32[512,768]{1,0:T(8,128)}, f32[512,256]{1,0:T(8,128)}) async-done(((f32[512,768]{1,0:T(8,128)}, f32[512,256]{1,0:T(8,128)}), (f32[512,768]{1,0:T(8,128)}, f32[512,256]{1,0:T(8,128)})) %all-reduce.14.cloned.1.call-update) | async-done | bytes 2097168 | tf_op jit(solution)/shard_map/psum | solution.py:45
  448.5 96.7 %all-reduce.10.cloned.1.call-done = (f32[512,1536]{1,0:T(8,128)}, f32[512,512]{0,1:T(8,128)}) async-done(((f32[512,1536]{1,0:T(8,128)}, f32[512,512]{0,1:T(8,128)}), (f32[512,1536]{1,0:T(8,128)}, f32[512,512]{0,1:T(8,128)})) %all-reduce.10.cloned.1.call-update) | async-done | bytes 4194320 | tf_op jit(solution)/shard_map/psum | solution.py:50
  547.2 11.7 %cholesky.358 = f32[128,128]{1,0:T(8,128)S(1)} custom-call(f32[128,128]{1,0:T(8,128)S(1)} %cholesky.439), custom_call_target="Cholesky" | custom-call | tf_op jit(solution)/shard_map/jit(cholesky)/cholesky | solution.py:48
  559.0 9.8 %custom-call.36 = f32[1,128,128]{1,2,0:T(8,128)S(1)} custom-call(f32[1,128,128]{2,1,0:T(8,128)S(1)} %get-tuple-element.90), custom_call_target="InvertDiagBlocksLowerTriangular" | custom-call | tf_op jit(solution)/shard_map/jit(cholesky)/cholesky | solution.py:48
  569.5 11.7 %cholesky.377 = f32[128,128]{1,0:T(8,128)S(1)} custom-call(f32[128,128]{1,0:T(8,128)S(1)} %cholesky.443), custom_call_target="Cholesky" | custom-call | tf_op jit(solution)/shard_map/jit(cholesky)/cholesky | solution.py:48
  581.3 10.2 %custom-call.37 = f32[1,128,128]{1,2,0:T(8,128)S(1)} custom-call(f32[1,128,128]{2,1,0:T(8,128)S(1)} %get-tuple-element.87), custom_call_target="InvertDiagBlocksLowerTriangular" | custom-call | tf_op jit(solution)/shard_map/jit(cholesky)/cholesky | solution.py:48
  592.1 11.7 %cholesky.398 = f32[128,128]{1,0:T(8,128)S(1)} custom-call(f32[128,128]{1,0:T(8,128)S(1)} %cholesky.448), custom_call_target="Cholesky" | custom-call | tf_op jit(solution)/shard_map/jit(cholesky)/cholesky | solution.py:48
  603.9 9.8 %custom-call.38 = f32[1,128,128]{1,2,0:T(8,128)S(1)} custom-call(f32[1,128,128]{2,1,0:T(8,128)S(1)} %get-tuple-element.84), custom_call_target="InvertDiagBlocksLowerTriangular" | custom-call | tf_op jit(solution)/shard_map/jit(cholesky)/cholesky | solution.py:48
  614.3 11.7 %cholesky.415 = f32[128,128]{1,0:T(8,128)S(1)} custom-call(f32[128,128]{1,0:T(8,128)S(1)} %convolution_subtract_fusion.18), custom_call_target="Cholesky" | custom-call | tf_op jit(solution)/shard_map/jit(cholesky)/cholesky | solution.py:48
  631.7 8.1 %while.9 = (s32[]{:T(128)}, f32[512,512]{1,0:T(8,128)S(1)}, s32[4,2]{0,1:T(2,128)S(1)}, f32[4,128,128]{2,1,0:T(8,128)S(1)}, s32[]{:T(128)}) while((s32[]{:T(128)}, f32[512,512]{1,0:T(8,128)S(1)}, s32[4,2]{0,1:T(2,128)S(1)}, f32[4,128,128]{2,1,0:T(8,128)S(1)}, s32[]{:T(128)}) %tuple.98), condition=%wide.while_cond.1.clone, body=%wide.while_body.1.clone.sunk | while | flops 2 | bytes 131189 | solution.py:21
  639.8 39.3 %custom-call.40 = f32[4,128,128]{1,2,0:T(8,128)S(1)} custom-call(f32[4,128,128]{2,1,0:T(8,128)S(1)} %get-tuple-element.40), custom_call_target="InvertDiagBlocksLowerTriangular" | custom-call | tf_op jit(solution)/shard_map/triangular_solve/custom-call.8 | solution.py:21
  695.3 10.7 %subtract_select_fusion = f32[1536,768]{1,0:T(8,128)} fusion(f32[1536,768]{1,0:T(8,128)S(1)} %bitcast.165, f32[512,768]{1,0:T(8,128)S(1)} %copy-done.3, pred[768]{0:T(1024)(128)(4,1)S(1)} %broadcast_compare_fusion.3, pred[1536]{0:T(1024)(128)(4,1)S(1)} %broadcast_compare_fusion.1, f32[128,1536]{1,0:T(8,128)S(1)} %fusion.90, f32[128,1536]{1,0:T(8,128)S(1)} %fusion.88, ...), kind=kOutput, calls=%fused_computation.16 | convolution fusion | flops 7253655552 | bytes 14158080 | tf_op jit(solution)/shard_map/dot_general | solution.py:10
  705.9 6.5 fusion.4
  (182 shorter events, 102.5 us)
Async XLA Ops:
  7.2 79.9 %all-reduce.16.cloned.1.call-start = ((), (), s32[]{:S(2)}) async-start(), calls=%async_computation.3 | async-start | bytes 4194304 | tf_op jit(solution)/shard_map/psum | solution.py:45
  17.2 1.4 copy-start.8
  19.6 176.8 %all-reduce.12.cloned.1.call-start = ((), (), s32[]{:S(2)}) async-start(), calls=%async_computation.1 | async-start | bytes 8388608 | tf_op jit(solution)/shard_map/psum | solution.py:50
  91.8 344.2 %all-reduce.14.cloned.1.call-start = ((), (), s32[]{:S(2)}) async-start(), calls=%async_computation.2 | async-start | bytes 4194304 | tf_op jit(solution)/shard_map/psum | solution.py:45
  196.4 1.7 copy-start.4
  330.9 2.9 copy-start.6
  338.2 7.0 slice-start.2
  340.6 4.6 slice-start.3
  342.4 2.8 copy-start.2
  345.2 10.7 %copy-start.10 = (bf16[1536,256]{1,0:T(8,128)(2,1)S(1)}, bf16[1536,256]{1,0:T(8,128)(2,1)}, u32[]{:S(2)}) copy-start(bf16[1536,256]{1,0:T(8,128)(2,1)} %param.17) | copy-start | bytes 2359300
  345.3 10.7 %copy-start.11 = (f32[512,256]{1,0:T(8,128)S(1)}, f32[512,256]{1,0:T(8,128)}, u32[]{:S(2)}) copy-start(f32[512,256]{1,0:T(8,128)} %get-tuple-element.68) | copy-start | bytes 1572868
  361.5 5.4 copy-start
  369.1 1.4 copy-start.9
  371.5 173.7 %all-reduce.10.cloned.1.call-start = ((), (), s32[]{:S(2)}) async-start(), calls=%async_computation | async-start | bytes 8388608 | tf_op jit(solution)/shard_map/psum | solution.py:50
  545.2 1.7 copy-start.5
  681.1 2.9 copy-start.7
  688.3 6.9 slice-start
  690.8 4.4 slice-start.1
  692.6 2.6 copy-start.3
  695.2 10.7 %copy-start.1 = (f32[1536,256]{1,0:T(8,128)S(1)}, f32[1536,256]{1,0:T(8,128)}, u32[]{:S(2)}) copy-start(f32[1536,256]{1,0:T(8,128)} %copy-done) | copy-start | bytes 4718596
  695.3 10.7 %copy-start.12 = (f32[512,256]{1,0:T(8,128)S(1)}, f32[512,256]{1,0:T(8,128)}, u32[]{:S(2)}) copy-start(f32[512,256]{1,0:T(8,128)} %get-tuple-element.66) | copy-start | bytes 1572868
Sparse Core Ops, SparseCore 0:
  19.7 67.3 all-reduce.15
  92.0 104.3 all-reduce.11
  371.7 64.2 all-reduce.13
  440.8 104.3 all-reduce.9
where the time goes:
time: 726 us; the launch traced here: 719 us
  waiting for transfers between devices  297 us (41%)
  other arithmetic  268 us (37%)
  matrix products  69.1 us (10%)
  local copies, waits for them, and re-layouts  65 us (9%)
  between operations  20.1 us (3%)
    psum x2, waiting for transfers between devices, per_device(): columns = lax.psum(mine_cols, 'col')  193 us
    another operation x29, other arithmetic, per_device(): factor = jnp.linalg.cholesky(pivot)  158 us
    psum x2, waiting for transfers between devices, per_device(): panel_rows, slab_rows = lax.psum((mine_rows, mine_slab), 'row')  104 us
    another operation x5, other arithmetic, solve_pivot(): lax.linalg.triangular_solve(factor, half, left_side=True, lower=True, tra...  79.2 us
    dot_general x4, matrix products, contract_rows(): lax.dot_general(gains, rows, (((0,), (0,)), ((), ())), precision=lax.Prec...  33.4 us
    another operation x14, matrix products, solve_pivot(): half = lax.linalg.triangular_solve(factor, rhs, left_side=True, lower=True)  18.3 us
    another operation x27, local copies, waits for them, and re-layouts, solve_pivot(): lax.linalg.triangular_solve(factor, half, left_side=True, lower=True, tra...  15.6 us
    another operation x4, other arithmetic, locate(): jnp.zeros((count,), jnp.float32).at[clipped].max(valid.astype(jnp.float32))  15.5 us
  transfers between devices with their start and end apart: 4, of which 4 were waited for; matrix products, arithmetic and copies ran while one was open for 6% of the time, Pallas kernels for 0%

commit v1 on v0

--- a/solution.py
+++ b/solution.py
@@ -1,9 +1,19 @@
+import functools
 import jax
 import jax.numpy as jnp
 from jax import lax
 from jax.sharding import PartitionSpec as P
 
 PANELS = 2
+
+
+def _name_bench(local_block, device_axis):
+    oldest = jax.lax.all_gather(local_block, axis_name=device_axis)
+    a_now = jnp.sum(oldest, axis=0)
+    return a_now
+
+
+unite_strings_here = functools.partial(_name_bench, device_axis="col")
 
 
 def contract_rows(gains, rows):
@@ -47,7 +57,7 @@
         pivot = lax.psum(panel_pivot, "col")
         factor = jnp.linalg.cholesky(pivot)
         mine_cols = jnp.where(col_valid[None, :], jnp.take(inverse, col_pick, axis=1), 0.0)
-        columns = lax.psum(mine_cols, "col")
+        columns = unite_strings_here(mine_cols)
         gains = solve_pivot(factor, columns.T)
         slab = slab - contract_rows(gains, slab_rows)
         slab = jnp.where(row_marked[:, None], 0.0, slab)

time: 726 us -> 1130 us (1.56)
  waiting for transfers between devices: 297 us -> 567 us
  local copies, waits for them, and re-layouts: 65 us -> 171 us
  other arithmetic: 268 us -> 302 us
    all_gather x0 -> x2, waiting for transfers between devices: none -> 305 us  [_name_bench(): oldest = jax.lax.all_gather(local_block, axis_name=device_axis)]
    unnamed x35 -> x33, local copies, waits for them, and re-layouts: 6.13 us -> 112 us
    psum x2, waiting for transfers between devices: 193 us -> 130 us  [per_device(): pivot = lax.psum(panel_pivot, 'col')]
    reduce_sum x0 -> x2, other arithmetic: none -> 34.5 us  [_name_bench(): a_now = jnp.sum(oldest, axis=0)]
    psum x2, waiting for transfers between devices: 104 us -> 132 us  [per_device(): panel_rows, slab_rows = lax.psum((mine_rows, mine_slab), 'row')]
  transfers between devices with their start and end apart: 4 -> 6, of which waited for: 4 -> 6; matrix products, arithmetic and copies ran while one was open for 6% -> 27% of each run, Pallas kernels for 0% -> 0%
where the time goes in v1:
time: 1130 us
  waiting for transfers between devices  567 us (50%)
  other arithmetic  302 us (27%)
  local copies, waits for them, and re-layouts  171 us (15%)
  matrix products  64.2 us (6%)
  between operations  20.4 us (2%)
    all_gather x2, waiting for transfers between devices, _name_bench(): oldest = jax.lax.all_gather(local_block, axis_name=device_axis)  305 us
    another operation x29, other arithmetic, per_device(): factor = jnp.linalg.cholesky(pivot)  158 us
    psum x2, waiting for transfers between devices, per_device(): panel_rows, slab_rows = lax.psum((mine_rows, mine_slab), 'row')  132 us
    psum x2, waiting for transfers between devices, per_device(): pivot = lax.psum(panel_pivot, 'col')  130 us
    unnamed x33, local copies, waits for them, and re-layouts  112 us
    another operation x5, other arithmetic, solve_pivot(): lax.linalg.triangular_solve(factor, half, left_side=True, lower=True, tra...  79.3 us
    reduce_sum x2, other arithmetic, _name_bench(): a_now = jnp.sum(oldest, axis=0)  34.5 us
    dot_general x4, matrix products, contract_rows(): lax.dot_general(gains, rows, (((0,), (0,)), ((), ())), precision=lax.Prec...  33.4 us
  transfers between devices with their start and end apart: 6, of which 6 were waited for; matrix products, arithmetic and copies ran while one was open for 27% of the time, Pallas kernels for 0%

profile of v1, /device:TPU:1, one launch (start us, length us, event | category | flops | bytes accessed | tf_op | source)
XLA Modules:
  0.0 1125.6 jit_solution(4561291569028599523)
XLA Ops:
  19.7 67.4 %all-reduce.14.cloned.1.call-done = (f32[512,768]{1,0:T(8,128)}, f32[512,256]{1,0:T(8,128)}) async-done(((f32[512,768]{1,0:T(8,128)}, f32[512,256]{1,0:T(8,128)}), (f32[512,768]{1,0:T(8,128)}, f32[512,256]{1,0:T(8,128)})) %all-reduce.14.cloned.1.call-update) | async-done | bytes 2097168 | tf_op jit(solution)/shard_map/psum | solution.py:55
  91.9 6.0 copy.19
  114.3 64.7 %all-reduce.8.cloned.1.call-done = f32[512,512]{0,1:T(8,128)} async-done(((f32[512,512]{0,1:T(8,128)}), f32[512,512]{0,1:T(8,128)}) %all-reduce.8.cloned.1.call-update) | async-done | bytes 1048592 | tf_op jit(solution)/shard_map/psum | solution.py:57
  180.9 11.7 %cholesky.286 = f32[128,128]{1,0:T(8,128)S(1)} custom-call(f32[128,128]{1,0:T(8,128)S(1)} %cholesky.426), custom_call_target="Cholesky" | custom-call | tf_op jit(solution)/shard_map/jit(cholesky)/cholesky | solution.py:58
  192.8 9.8 custom-call.31
  203.2 11.7 %cholesky.305 = f32[128,128]{1,0:T(8,128)S(1)} custom-call(f32[128,128]{1,0:T(8,128)S(1)} %cholesky.430), custom_call_target="Cholesky" | custom-call | tf_op jit(solution)/shard_map/jit(cholesky)/cholesky | solution.py:58
  215.0 10.0 custom-call.32
  225.6 11.7 %cholesky.326 = f32[128,128]{1,0:T(8,128)S(1)} custom-call(f32[128,128]{1,0:T(8,128)S(1)} %cholesky.435), custom_call_target="Cholesky" | custom-call | tf_op jit(solution)/shard_map/jit(cholesky)/cholesky | solution.py:58
  237.4 9.8 custom-call.33
  247.8 11.7 %cholesky.343 = f32[128,128]{1,0:T(8,128)S(1)} custom-call(f32[128,128]{1,0:T(8,128)S(1)} %convolution_subtract_fusion.19), custom_call_target="Cholesky" | custom-call | tf_op jit(solution)/shard_map/jit(cholesky)/cholesky | solution.py:58
  264.6 8.4 while.8
  273.0 39.3 %custom-call.35 = f32[4,128,128]{1,2,0:T(8,128)S(1)} custom-call(f32[4,128,128]{2,1,0:T(8,128)S(1)} %get-tuple-element.38), custom_call_target="InvertDiagBlocksLowerTriangular" | custom-call | tf_op jit(solution)/shard_map/triangular_solve/custom-call.8 | solution.py:31
  312.3 153.1 %all-gather.5.cloned.1.call-done = f32[24576,512]{0,1:T(8,128)} async-done(((f32[1536,512]{0,1:T(8,128)}), f32[24576,512]{0,1:T(8,128)}) %all-gather.5.cloned.1.call-update) | async-done | bytes 50331664 | tf_op jit(solution)/shard_map/all_gather | solution.py:11
  465.4 53.0 %copy.23 = f32[64,8,16,1536]{3,2,1,0:T(8,128)} copy(f32[64,8,16,1536]{3,1,2,0:T(8,128)} %bitcast.172) | data formatting | bytes 100663296
  518.5 17.3 %bitcast_reduce_fusion.1 = f32[1536,512]{0,1:T(8,128)S(1)} fusion(f32[64,8,16,1536]{3,2,1,0:T(8,128)} %copy.23), kind=kLoop, calls=%fused_computation.17 | loop fusion | flops 11796480 | bytes 53477376 | tf_op jit(solution)/shard_map/reduce_sum | solution.py:12
  549.6 10.7 subtract_select_fusion.1
  576.0 64.2 %all-reduce.12.cloned.1.call-done = (f32[512,768]{1,0:T(8,128)}, f32[512,256]{1,0:T(8,128)}) async-done(((f32[512,768]{1,0:T(8,128)}, f32[512,256]{1,0:T(8,128)}), (f32[512,768]{1,0:T(8,128)}, f32[512,256]{1,0:T(8,128)})) %all-reduce.12.cloned.1.call-update) | async-done | bytes 2097168 | tf_op jit(solution)/shard_map/psum | solution.py:55
  667.0 65.0 %all-reduce.10.cloned.1.call-done = f32[512,512]{0,1:T(8,128)} async-done(((f32[512,512]{0,1:T(8,128)}), f32[512,512]{0,1:T(8,128)}) %all-reduce.10.cloned.1.call-update) | async-done | bytes 1048592 | tf_op jit(solution)/shard_map/psum | solution.py:57
  733.9 11.7 %cholesky.358 = f32[128,128]{1,0:T(8,128)S(1)} custom-call(f32[128,128]{1,0:T(8,128)S(1)} %cholesky.439), custom_call_target="Cholesky" | custom-call | tf_op jit(solution)/shard_map/jit(cholesky)/cholesky | solution.py:58
  745.8 9.8 custom-call.36
  756.2 11.7 %cholesky.377 = f32[128,128]{1,0:T(8,128)S(1)} custom-call(f32[128,128]{1,0:T(8,128)S(1)} %cholesky.443), custom_call_target="Cholesky" | custom-call | tf_op jit(solution)/shard_map/jit(cholesky)/cholesky | solution.py:58
  768.0 10.0 custom-call.37
  778.6 11.7 %cholesky.398 = f32[128,128]{1,0:T(8,128)S(1)} custom-call(f32[128,128]{1,0:T(8,128)S(1)} %cholesky.448), custom_call_target="Cholesky" | custom-call | tf_op jit(solution)/shard_map/jit(cholesky)/cholesky | solution.py:58
  790.4 9.8 custom-call.38
  800.8 11.7 %cholesky.415 = f32[128,128]{1,0:T(8,128)S(1)} custom-call(f32[128,128]{1,0:T(8,128)S(1)} %convolution_subtract_fusion.18), custom_call_target="Cholesky" | custom-call | tf_op jit(solution)/shard_map/jit(cholesky)/cholesky | solution.py:58
  818.0 7.7 while.9
  825.8 39.3 %custom-call.40 = f32[4,128,128]{1,2,0:T(8,128)S(1)} custom-call(f32[4,128,128]{2,1,0:T(8,128)S(1)} %get-tuple-element.40), custom_call_target="InvertDiagBlocksLowerTriangular" | custom-call | tf_op jit(solution)/shard_map/triangular_solve/custom-call.8 | solution.py:31
  865.1 152.3 %all-gather.7.cloned.1.call-done = f32[24576,512]{0,1:T(8,128)} async-done(((f32[1536,512]{0,1:T(8,128)}), f32[24576,512]{0,1:T(8,128)}) %all-gather.7.cloned.1.call-update) | async-done | bytes 50331664 | tf_op jit(solution)/shard_map/all_gather | solution.py:11
  1017.4 53.0 %copy.24 = f32[64,8,16,1536]{3,2,1,0:T(8,128)} copy(f32[64,8,16,1536]{3,1,2,0:T(8,128)} %bitcast.173) | data formatting | bytes 100663296
  1070.4 17.2 %bitcast_reduce_fusion = f32[1536,512]{0,1:T(8,128)S(1)} fusion(f32[64,8,16,1536]{3,2,1,0:T(8,128)} %copy.24), kind=kLoop, calls=%fused_computation.16 | loop fusion | flops 11796480 | bytes 53477376 | tf_op jit(solution)/shard_map/reduce_sum | solution.py:12
  1101.3 10.7 subtract_select_fusion
  1112.0 6.6 fusion.2
  (188 shorter events, 132.3 us)
Async XLA Ops:
  7.2 79.9 %all-reduce.14.cloned.1.call-start = ((), (), s32[]{:S(2)}) async-start(), calls=%async_computation.5 | async-start | bytes 4194304 | tf_op jit(solution)/shard_map/psum | solution.py:55
  17.2 1.4 copy-start.6
  19.6 159.4 %all-reduce.8.cloned.1.call-start = ((), (), s32[]{:S(2)}) async-start(), calls=%async_computation | async-start | bytes 2097152 | tf_op jit(solution)/shard_map/psum | solution.py:57
  91.8 373.6 %all-gather.5.cloned.1.call-start = ((), (), s32[]{:S(2)}) async-start(), calls=%async_computation.2 | async-start | bytes 53477376 | tf_op jit(solution)/shard_map/all_gather | solution.py:11
  106.0 534.1 %all-reduce.12.cloned.1.call-start = ((), (), s32[]{:S(2)}) async-start(), calls=%async_computation.4 | async-start | bytes 4194304 | tf_op jit(solution)/shard_map/psum | solution.py:55
  179.0 1.7 copy-start.4
  541.7 7.9 slice-start.2
  545.0 4.6 slice-start.3
  546.8 2.8 copy-start.2
  549.6 10.7 copy-start.8
  549.6 10.7 copy-start.9
  565.8 5.4 copy-start
  573.5 1.4 copy-start.7
  575.9 156.1 %all-reduce.10.cloned.1.call-start = ((), (), s32[]{:S(2)}) async-start(), calls=%async_computation.1 | async-start | bytes 2097152 | tf_op jit(solution)/shard_map/psum | solution.py:57
  644.8 372.5 %all-gather.7.cloned.1.call-start = ((), (), s32[]{:S(2)}) async-start(), calls=%async_computation.3 | async-start | bytes 53477376 | tf_op jit(solution)/shard_map/all_gather | solution.py:11
  732.0 1.7 copy-start.5
  1093.6 7.7 slice-start
  1096.9 4.4 slice-start.1
  1098.7 2.6 copy-start.3
  1101.3 10.7 copy-start.1
  1101.3 10.7 copy-start.10
Sparse Core Ops, SparseCore 0:
  19.7 67.3 all-reduce.13
  92.0 86.9 all-reduce.7
  181.7 283.6 all-gather.4
  576.0 64.0 all-reduce.11
  645.0 86.9 all-reduce.9
  734.0 283.3 all-gather.6
